TPU v7x, 512 devices: a whole 4x4x16 slice. The times are simulated.
512 devices in a mesh: pipe: 16 (over z_lo, y), dp: 32 (over z_hi, x, core).
Axes of the slice: x: 4, y: 4, z: 16 (z_hi: 4, z_lo: 4; z = z_hi * 4 + z_lo), core: 2. Of those that a mesh axis runs over, the one named last changes fastest.
Arguments:
- queries: bfloat16 [16, 4096, 4096], P('pipe', 'dp'), may hold values from -6 to 6
- out_grad: bfloat16 [16, 4096, 4096], P('pipe', 'dp'), may hold values from -6 to 6
- keys: bfloat16 [16, 2048, 512], P('pipe', 'dp'), may hold values from -6 to 6
- values: bfloat16 [16, 2048, 512], P('pipe', 'dp'), may hold values from -6 to 6
- kv_weight: bfloat16 [16, 8192, 1024], P('pipe', 'dp'), may hold values from -0.0625 to 0.0625
- stream: bfloat16 [2048, 8192], P(None, 'dp'), may hold values from -640 to 640
- norm_gain: float32 [8192], P('dp'), may hold values from 0.1 to 1.9
- lengths: int32 [32], P('dp'), may hold values from 32 to 128, as said below
Outputs:
- kv_weight_grad: float32 [16, 8192, 1024], P('pipe', 'dp')
- latent_grad: bfloat16 [2048, 8192], P('pipe', 'dp')
- gain_grad: float32 [8192], P('dp')
Inputs may be any that keep to these rules, and one draw needn't show every extreme that they name: `lengths`: each micro-batch has 32 to 128 live tokens; some micro-batch has exactly 128 and another exactly 32.
All inputs are finite; a program needn't handle non-finite values.
Results may differ from a plain program's by a relative error of at most 0.0057.
Values may be sent and summed in bfloat16 or wider, within the bound.
A program may use at most 64 MiB of HBM per device.

v0:
```python
import math
import jax
import jax.numpy as jnp
from jax import lax
from jax.sharding import PartitionSpec as P

D = 8192
HQ = 32
KVH = 4
HD = 128
NORM_EPS = 1e-05


def attention_grads(query_rows, grad_rows, key_rows, value_rows, length):
    token_count = query_rows.shape[0]
    latent_count = key_rows.shape[0]
    group_size = HQ // KVH
    score_scale = 1.0 / math.sqrt(HD)
    token_live = lax.iota(jnp.int32, token_count) < length
    masked = jnp.where(token_live[:, None], grad_rows, jnp.zeros_like(grad_rows))
    query_h = query_rows.reshape(token_count, KVH, group_size, HD)
    grad_h = masked.reshape(token_count, KVH, group_size, HD)
    key_h = key_rows.reshape(latent_count, KVH, HD)
    value_h = value_rows.reshape(latent_count, KVH, HD)
    scores = (
        jnp.einsum("tgqd,jgd->gqjt", query_h, key_h, preferred_element_type=jnp.float32)
        * score_scale
    )
    row_max = jnp.max(scores, axis=2, keepdims=True)
    expo = jnp.exp(scores - row_max)
    prob_values = expo / jnp.sum(expo, axis=2, keepdims=True)
    dprob = jnp.einsum("tgqd,jgd->gqjt", grad_h, value_h, preferred_element_type=jnp.float32)
    centre = jnp.sum(prob_values * dprob, axis=2, keepdims=True)
    dscore = (prob_values * (dprob - centre) * score_scale).astype(jnp.bfloat16)
    probs_b = prob_values.astype(jnp.bfloat16)
    key_grad = jnp.einsum("gqjt,tgqd->jgd", dscore, query_h, preferred_element_type=jnp.float32)
    value_grad = jnp.einsum("gqjt,tgqd->jgd", probs_b, grad_h, preferred_element_type=jnp.float32)
    joined = jnp.concatenate(
        [key_grad.reshape(latent_count, KVH * HD), value_grad.reshape(latent_count, KVH * HD)],
        axis=1,
    )
    return joined.astype(jnp.bfloat16)


def body(queries, out_grad, keys, values, kv_weight, stream, norm_gain, lengths):
    kv_grads = attention_grads(queries[0], out_grad[0], keys[0], values[0], lengths[0])
    promoted = stream.astype(jnp.float32)
    squares = lax.psum(jnp.sum(promoted * promoted, axis=1), "dp")
    inverse = lax.rsqrt(squares / D + NORM_EPS)[:, None]
    normed = promoted * inverse
    latents = (normed * norm_gain[None, :]).astype(jnp.bfloat16)
    gathered = lax.all_gather(kv_grads, "dp", axis=0, tiled=True)
    group_total = lax.axis_size("dp")
    weight = kv_weight[0]
    weight_grad = (
        lax.dot_general(
            latents, gathered, (((0,), (0,)), ((), ())), preferred_element_type=jnp.float32
        )
        / group_total
    )
    row_count = gathered.shape[0] // lax.axis_size("pipe")
    first_row = lax.axis_index("pipe") * row_count
    share_rows = lax.psum_scatter(
        lax.dot_general(
            gathered, weight, (((1,), (1,)), ((), ())), preferred_element_type=jnp.float32
        ),
        "pipe",
        scatter_dimension=0,
        tiled=True,
    )
    normed_share = lax.dynamic_slice_in_dim(normed, first_row, row_count, 0)
    gain_part = jnp.sum(share_rows * normed_share, axis=0)
    gain_grad = lax.psum(gain_part, "pipe") / group_total
    return (weight_grad[None], share_rows.astype(jnp.bfloat16), gain_grad)


def solution(mesh):
    return jax.shard_map(
        body,
        mesh=mesh,
        in_specs=(
            P("pipe", "dp", None),
            P("pipe", "dp", None),
            P("pipe", "dp", None),
            P("pipe", "dp", None),
            P("pipe", "dp", None),
            P(None, "dp"),
            P("dp"),
            P("dp"),
        ),
        out_specs=(P("pipe", "dp", None), P("pipe", "dp"), P("dp")),
        check_vma=False,
    )
```

profile of v0, /device:TPU:128, one launch (start us, length us, event | category | flops | bytes accessed | tf_op | source)
XLA Modules:
  0.0 271.0 jit_solution(11565212643555635086)
XLA Ops:
  7.2 0.0 copy-start
  7.2 0.0 copy-start.3
  7.2 0.0 all-gather.2.cloned.1.call-start
  7.2 1.5 copy.33
  8.7 0.0 copy-done.3
  8.8 0.0 copy-start.2
  8.8 0.5 fusion.9
  9.3 0.0 copy-start.4
  9.3 1.2 fusion.32
  10.5 0.0 copy-done.2
  10.5 1.2 copy.34
  12.4 0.0 copy-done.4
  12.4 2.8 %convolution_bitcast_fusion = f32[4,8,64,128]{3,2,1,0:T(8,128)} fusion(bf16[128,4,8,128]{3,2,1,0:T(8,128)(2,1)} %bitcast.53, pred[128]{0:T(512)(128)(4,1)S(1)} %iota_compare_fusion, bf16[64,4,128,1]{2,1,0,3:T(4,128)(2,1)S(1)} %bitcast.56), kind=kOutput, calls=%fused_computation.13 | convolution fusion | flops 67633152 | bytes 2162816 | tf_op jit(solution)/shard_map/tgqd,jgd->gqjt/dot_general | solution.py:32
  15.2 1.9 fusion.15
  17.2 2.9 %fusion.16 = bf16[4,8,8,128]{3,2,1,0:T(8,128)(2,1)S(1)} fusion(f32[4,8,64,128]{3,2,1,0:T(8,128)} %convolution_bitcast_fusion, bf16[128,4,8,128]{3,2,1,0:T(8,128)(2,1)S(1)} %bitcast.50, f32[4,8,64,128]{3,2,1,0:T(8,128)} %get-tuple-element.6, f32[4,8,128]{2,1,0:T(8,128)S(1)} %get-tuple-element.5), kind=kOutput, calls=%fused_computation.23 | convolution fusion | flops 68980800 | bytes 3227648 | tf_op jit(solution)/shard_map/gqjt,tgqd->jgd/dot_general | solution.py:36
  20.1 0.7 pad_maximum_fusion
  20.8 0.0 all-gather.2.cloned.1.call-update
  20.8 0.0 reduce-scatter.2.cloned.1.call-start
  20.9 94.6 %all-gather.2.cloned.1.call-done = bf16[2048,1024]{1,0:T(8,128)(2,1)} async-done(((bf16[64,1024]{1,0:T(8,128)(2,1)}), bf16[2048,1024]{1,0:T(8,128)(2,1)}) %all-gather.2.cloned.1.call-update) | async-done | bytes 4194320 | tf_op jit(solution)/shard_map/all_gather | solution.py:52
  115.5 0.0 copy-done
  115.5 4.8 %fusion.22 = f32[2048,256]{1,0:T(8,128)} fusion(bf16[2048,1024]{1,0:T(8,128)(2,1)} %all-gather.2.cloned.1.call-done, bf16[1,256,1024]{2,1,0:T(8,128)(2,1)S(1)} %copy-done), kind=kOutput, calls=%fused_computation.30 | convolution fusion | flops 1073741824 | bytes 6815744 | tf_op jit(solution)/shard_map/dot_general | solution.py:64
  120.3 0.0 copy-start.1
  120.3 0.0 reduce-scatter.2.cloned.1.call-update
  120.4 1.2 copy-done.1
  121.6 0.0 copy-start.5
  121.6 0.3 fusion.2
  121.9 91.9 %psum.14 = f32[2048]{0:T(1024)S(1)} all-reduce(f32[2048]{0:T(1024)S(1)} %fusion.2), channel_id=1, replica_groups=mesh['pipe'=16,'dp'=32] {'dp'}, use_global_device_ids=true, to_apply=%region_1.2 | all-reduce | flops 2048 | bytes 16384 | tf_op jit(solution)/shard_map/psum | solution.py:48
  213.8 1.7 convert_multiply_fusion
  215.5 0.0 copy-done.5
  215.5 4.5 %fusion.8 = f32[1,256,1024]{2,1,0:T(8,128)} fusion(bf16[2048,1024]{1,0:T(8,128)(2,1)} %all-gather.2.cloned.1.call-done, f32[256]{0:T(256)S(1)} %copy-done.5, bf16[2048,256]{1,0:T(8,128)(2,1)S(1)} %copy-done.1, f32[2048]{0:T(1024)S(1)} %add_rsqrt_fusion), kind=kOutput, calls=%fused_computation.12 | convolution fusion | flops 1076101120 | bytes 6300672 | tf_op jit(solution)/shard_map/dot_general | solution.py:56
  220.0 0.0 reduce-scatter.2.cloned.1.call-done
  220.0 1.7 multiply_reduce_fusion.1
  221.7 41.9 %psum.15 = f32[256]{0:T(256)S(1)} all-reduce(f32[256]{0:T(256)S(1)} %get-tuple-element.3), channel_id=1, replica_groups=mesh['pipe'=16,'dp'=32] {'pipe'}, use_global_device_ids=true, to_apply=%region_7.8 | all-reduce | flops 256 | bytes 2048 | tf_op jit(solution)/shard_map/psum | solution.py:73
  263.6 0.6 broadcast_multiply_fusion
  (5 shorter events, 0.1 us)
Async XLA Ops:
  7.2 108.4 %copy-start = (bf16[1,256,1024]{2,1,0:T(8,128)(2,1)S(1)}, bf16[1,256,1024]{2,1,0:T(8,128)(2,1)}, u32[]{:S(2)}) copy-start(bf16[1,256,1024]{2,1,0:T(8,128)(2,1)} %param.12) | copy-start | bytes 1572868
  7.2 1.6 copy-start.3
  7.2 108.3 %all-gather.2.cloned.1.call-start = ((), (), s32[]{:S(2)}) async-start(), calls=%async_computation.1 | async-start | bytes 4325376 | tf_op jit(solution)/shard_map/all_gather | solution.py:52
  8.8 1.7 copy-start.2
  9.3 3.1 %copy-start.4 = (bf16[1,64,512]{2,1,0:T(8,128)(2,1)S(1)}, bf16[1,64,512]{2,1,0:T(8,128)(2,1)}, u32[]{:S(2)}) copy-start(bf16[1,64,512]{2,1,0:T(8,128)(2,1)} %param.11) | copy-start | bytes 196612
  20.8 199.2 %reduce-scatter.2.cloned.1.call-start = ((), (), s32[]{:S(2)}) async-start(), calls=%async_computation.2 | async-start | bytes 2228224 | tf_op jit(solution)/shard_map/reduce_scatter | solution.py:63
  120.3 1.2 copy-start.1
  121.6 93.9 %copy-start.5 = (f32[256]{0:T(256)S(1)}, f32[256]{0:T(256)}, u32[]{:S(2)}) copy-start(f32[256]{0:T(256)} %param.14) | copy-start | bytes 3076
Sparse Core Ops, SparseCore 0:
  20.9 94.5 all-gather.1
  120.5 92.4 reduce-scatter.1
where the time goes:
time: 271 us
  blocking collectives  134 us (49%)
  waiting for transfers between devices  94.7 us (35%)
  matrix products  17.6 us (6%)
  between operations  14.8 us (5%)
  other arithmetic  6.15 us (2%)
  local copies, waits for them, and re-layouts  3.97 us (1%)
    all_gather x1, waiting for transfers between devices, body(): gathered = lax.all_gather(kv_grads, 'dp', axis=0, tiled=True)  94.6 us
    psum x1, blocking collectives, body(): squares = lax.psum(jnp.sum(promoted * promoted, axis=1), 'dp')  91.9 us
    psum x1, blocking collectives, body(): gain_grad = lax.psum(gain_part, 'pipe') / group_total  41.9 us
  transfers between devices with their start and end apart: 2, of which 1 were waited for; matrix products, arithmetic and copies ran while one was open for 2% of the time, Pallas kernels for 0%

commit v1 on v0

--- a/solution.py
+++ b/solution.py
@@ -49,7 +49,15 @@
     inverse = lax.rsqrt(squares / D + NORM_EPS)[:, None]
     normed = promoted * inverse
     latents = (normed * norm_gain[None, :]).astype(jnp.bfloat16)
-    gathered = lax.all_gather(kv_grads, "dp", axis=0, tiled=True)
+    gathered = jnp.concatenate(
+        lax.all_to_all(
+            jnp.stack(lax.axis_size("dp") * [kv_grads], axis=0),
+            axis_name="dp",
+            split_axis=0,
+            concat_axis=0,
+        ),
+        axis=0,
+    )
     group_total = lax.axis_size("dp")
     weight = kv_weight[0]
     weight_grad = (

time: 271 us -> 377 us (1.39)
  the two profiles are of different devices: /device:TPU:128 before, /device:TPU:16 now
where the time goes in v1:
time: 377 us
  blocking collectives  335 us (89%)
  matrix products  15.5 us (4%)
  between operations  14.8 us (4%)
  local copies, waits for them, and re-layouts  6.42 us (2%)
  other arithmetic  5.49 us (1%)
    all_to_all x1, blocking collectives, body(): lax.all_to_all(jnp.stack(lax.axis_size('dp') * [kv_grads], axis=0), axis_...  206 us
    psum x1, blocking collectives, body(): squares = lax.psum(jnp.sum(promoted * promoted, axis=1), 'dp')  89.8 us
    psum x1, blocking collectives, body(): gain_grad = lax.psum(gain_part, 'pipe') / group_total  39.1 us
  transfers between devices with their start and end apart: 1, of which 0 were waited for; matrix products, arithmetic and copies ran while one was open for 2% of the time, Pallas kernels for 0%

profile of v1, /device:TPU:16, one launch (start us, length us, event | category | flops | bytes accessed | tf_op | source)
XLA Modules:
  0.0 377.0 jit_solution(7771388425850751327)
XLA Ops:
  7.2 0.0 copy-start
  7.2 0.0 copy-start.4
  7.2 0.0 reduce-scatter.2.cloned.1.call-start
  7.2 1.5 copy.33
  8.7 0.0 copy-done.4
  8.8 0.0 copy-start.3
  8.8 0.5 fusion.9
  9.3 0.0 copy-start.5
  9.3 1.2 fusion.32
  10.5 0.0 copy-done.3
  10.5 1.2 copy.34
  12.4 0.0 copy-done.5
  12.4 2.8 convolution_bitcast_fusion
  15.3 1.9 fusion.15
  17.2 2.9 fusion.16
  20.2 0.5 stack.2
  20.7 205.9 %all_to_all.5 = bf16[32,64,1024]{2,1,0:T(8,128)(2,1)S(1)} all-to-all(bf16[32,64,1024]{2,1,0:T(8,128)(2,1)S(1)} %stack.2), channel_id=1, replica_groups=mesh['pipe'=16,'dp'=32] {'dp'}, dimensions={0} | all-to-all | bytes 8388608 | tf_op jit(solution)/shard_map/all_to_all | solution.py:53
  226.6 0.0 copy-start.2
  226.6 1.9 copy-done.2
  228.5 0.0 copy-done
  228.5 2.7 fusion.22
  231.3 0.0 copy-start.1
  231.3 0.0 reduce-scatter.2.cloned.1.call-update
  231.3 1.2 copy-done.1
  232.5 0.0 copy-start.6
  232.5 0.3 fusion.2
  232.8 89.8 %psum.14 = f32[2048]{0:T(1024)S(1)} all-reduce(f32[2048]{0:T(1024)S(1)} %fusion.2), channel_id=1, replica_groups=mesh['pipe'=16,'dp'=32] {'dp'}, use_global_device_ids=true, to_apply=%region_1.2 | all-reduce | flops 2048 | bytes 16384 | tf_op jit(solution)/shard_map/psum | solution.py:48
  322.6 1.7 convert_multiply_fusion
  324.3 0.0 copy-done.6
  324.3 4.5 %fusion.8 = f32[1,256,1024]{2,1,0:T(8,128)} fusion(bf16[2048,1024]{1,0:T(8,128)(2,1)} %bitcast.51, f32[256]{0:T(256)S(1)} %copy-done.6, bf16[2048,256]{1,0:T(8,128)(2,1)S(1)} %copy-done.1, f32[2048]{0:T(1024)S(1)} %add_rsqrt_fusion), kind=kOutput, calls=%fused_computation.12 | convolution fusion | flops 1076101120 | bytes 6300672 | tf_op jit(solution)/shard_map/dot_general | solution.py:64
  328.8 0.0 reduce-scatter.2.cloned.1.call-done
  328.8 1.7 multiply_reduce_fusion.1
  330.5 39.1 %psum.15 = f32[256]{0:T(256)S(1)} all-reduce(f32[256]{0:T(256)S(1)} %get-tuple-element.3), channel_id=1, replica_groups=mesh['pipe'=16,'dp'=32] {'pipe'}, use_global_device_ids=true, to_apply=%region_7.8 | all-reduce | flops 256 | bytes 2048 | tf_op jit(solution)/shard_map/psum | solution.py:81
  369.6 0.6 broadcast_multiply_fusion
  (6 shorter events, 0.1 us)
Async XLA Ops:
  7.2 221.4 %copy-start = (bf16[1,256,1024]{2,1,0:T(8,128)(2,1)S(1)}, bf16[1,256,1024]{2,1,0:T(8,128)(2,1)}, u32[]{:S(2)}) copy-start(bf16[1,256,1024]{2,1,0:T(8,128)(2,1)} %param.12) | copy-start | bytes 1572868
  7.2 1.6 copy-start.4
  7.2 321.7 %reduce-scatter.2.cloned.1.call-start = ((), (), s32[]{:S(2)}) async-start(), calls=%async_computation.2 | async-start | bytes 2228224 | tf_op jit(solution)/shard_map/reduce_scatter | solution.py:71
  8.8 1.7 copy-start.3
  9.3 3.1 copy-start.5
  226.6 1.9 copy-start.2
  231.3 1.2 copy-start.1
  232.5 91.8 %copy-start.6 = (f32[256]{0:T(256)S(1)}, f32[256]{0:T(256)}, u32[]{:S(2)}) copy-start(f32[256]{0:T(256)} %param.14) | copy-start | bytes 3076
Sparse Core Ops, SparseCore 0:
  231.4 83.3 reduce-scatter.1
